TPU v7x, 256 devices: a whole 4x4x8 slice. The times are simulated.
256 devices in a mesh: member: 8 (over y, x_hi), space: 32 (over z, x_lo, core).
Axes of the slice: x: 4 (x_hi: 2, x_lo: 2; x = x_hi * 2 + x_lo), y: 4, z: 8, core: 2. Of those that a mesh axis runs over, the one named last changes fastest.
Arguments:
- zonal_wind: bfloat16 [48, 256, 256, 128], P('member', 'space'), may hold values from -6 to 6
- meridional_wind: bfloat16 [48, 256, 256, 128], P('member', 'space'), may hold values from -6 to 6
- heat_anomaly: bfloat16 [48, 256, 256, 128], P('member', 'space'), may hold values from -6 to 6
- moisture_anomaly: bfloat16 [48, 256, 256, 128], P('member', 'space'), may hold values from -6 to 6
- projection_scale: float32 [256, 256], P('space'), may hold values from 0.5 to 2
- balance_multiplier: float32 [256, 256], P('space'), may hold values from -4 to 4
- heat_on_curl_slope: float32 [128], replicated, may hold values from 0.3 to 1.5
- moisture_on_heat_slope: float32 [128], replicated, may hold values from 0.3 to 1.5
Outputs:
- covariance: float32 [32, 512, 512], P('space', 'member')
All inputs are finite; a program needn't handle non-finite values.
Results may differ from a plain program's by a relative error of at most 0.0009.
Values may be sent and summed in bfloat16 or wider, within the bound.
No kernel may reach another device: no remote copies, remote signals or barrier semaphores. Data moves between devices by JAX's collectives and lax.ppermute only.
A program may use at most 128 MiB of HBM per device.

v0:
```python
import jax
import jax.numpy as jnp
from jax import lax
from jax.sharding import PartitionSpec as P


def extended(block, sides, width):
    for axis, dim in sides:
        count = lax.axis_size(axis)
        forward = [(i, i + 1) for i in range(count - 1)]
        backward = [(target, source) for source, target in forward]
        low = lax.ppermute(
            lax.slice_in_dim(block, block.shape[dim] - width, None, axis=dim), axis, forward
        )
        high = lax.ppermute(lax.slice_in_dim(block, 0, width, axis=dim), axis, backward)
        block = jnp.concatenate([low, block, high], axis=dim)
    return block


def lat_diff(padded):
    return (-padded[:, 4:] + 8.0 * padded[:, 3:-1] - 8.0 * padded[:, 1:-3] + padded[:, :-4]) / 12.0


def lon_diff(field):
    return (jnp.roll(field, -1, 2) - jnp.roll(field, 1, 2)) / 2.0


def gram_rows(left, right, precision):
    return lax.dot_general(
        left,
        right,
        (((0,), (0,)), ((), ())),
        preferred_element_type=jnp.float32,
        precision=precision,
    )


def on_device(
    zonal_wind,
    meridional_wind,
    heat_anomaly,
    moisture_anomaly,
    projection_scale,
    balance_multiplier,
    heat_on_curl_slope,
    moisture_on_heat_slope,
):
    winds = jnp.stack([zonal_wind, meridional_wind])
    padded = extended(winds, (("space", 2),), 2)
    u_full = padded[0].astype(jnp.float32)
    v_full = padded[1].astype(jnp.float32)
    u_mid = u_full[:, 2:-2]
    v_mid = v_full[:, 2:-2]
    factor = projection_scale[None, :, :, None]
    wind_curl = factor * (lon_diff(v_mid) - lat_diff(u_full))
    wind_spreading = factor * (lon_diff(u_mid) + lat_diff(v_full))
    heat_residual = (
        heat_anomaly.astype(jnp.float32)
        - heat_on_curl_slope * balance_multiplier[None, :, :, None] * wind_curl
    )
    moisture_residual = (
        moisture_anomaly.astype(jnp.float32) - moisture_on_heat_slope * heat_residual
    )
    sample_vector = jnp.concatenate(
        [wind_curl, wind_spreading, heat_residual, moisture_residual], axis=3
    ).astype(jnp.bfloat16)
    width = sample_vector.shape[3]
    groups = lax.axis_size("member")
    members_all = float(sample_vector.shape[0] * groups)
    rows = width // groups
    scale = 1.0 / (
        (sample_vector.shape[0] * groups - 1) * sample_vector.shape[1] * sample_vector.shape[2]
    )
    local_sum = jnp.sum(sample_vector.astype(jnp.float32), axis=0)
    highest = lax.Precision.HIGHEST
    totals = lax.psum(local_sum.astype(jnp.bfloat16), "member").astype(jnp.float32)
    ens_mean = totals / members_all
    anomaly = (sample_vector.astype(jnp.float32) - ens_mean[None]).reshape(-1, width)
    summed = lax.psum(gram_rows(anomaly, anomaly, highest), "member")
    mine = lax.dynamic_slice_in_dim(summed, lax.axis_index("member") * rows, rows, 0)
    return (mine * scale)[None]


def solution(mesh):
    placed = (
        P("member", "space", None, None),
        P("member", "space", None, None),
        P("member", "space", None, None),
        P("member", "space", None, None),
        P("space", None),
        P("space", None),
        P(),
        P(),
    )
    return jax.shard_map(
        on_device, mesh=mesh, in_specs=placed, out_specs=P("space", "member", None), check_vma=False
    )
```

profile of v0, /device:TPU:32, one launch (start us, length us, event | category | flops | bytes accessed | tf_op | source)
XLA Modules:
  0.0 398.0 jit_solution(15187263086016481652)
XLA Ops:
  6.5 0.0 all-reduce.3.cloned.1.call-start
  6.5 2.3 pad_maximum_fusion.4
  8.8 2.1 collective-permute-start
  10.9 4.5 %collective-permute-start.1 = (bf16[2,6,2,256,128]{4,3,2,1,0:T(8,128)(2,1)S(1)}, bf16[2,6,2,256,128]{4,3,2,1,0:T(8,128)(2,1)S(1)}, u32[]{:S(2)}, u32[]{:S(2)}) collective-permute-start(bf16[2,6,2,256,128]{4,3,2,1,0:T(8,128)(2,1)S(1)} %get-tuple-element.20), channel_id=1, source_target_pairs={{1,0},{2,1},{3,2},{4,3},{5,4},{6,5},{7,6},{8,7},{9,8},{10,9},{11,1... | collective-permute-start | bytes 4718600 | tf_op jit(solution)/shard_map/ppermute | solution.py:15
  15.4 0.0 copy-done.7
  15.4 0.0 copy-done.9
  15.5 1.3 broadcast_multiply_fusion
  16.8 14.9 %collective-permute-done = bf16[2,6,2,256,128]{4,3,2,1,0:T(8,128)(2,1)S(1)} collective-permute-done((bf16[2,6,2,256,128]{4,3,2,1,0:T(8,128)(2,1)S(1)}, bf16[2,6,2,256,128]{4,3,2,1,0:T(8,128)(2,1)S(1)}, u32[]{:S(2)}, u32[]{:S(2)}) %collective-permute-start) | collective-permute-done | bytes 1572896 | tf_op jit(solution)/shard_map/ppermute | solution.py:12
  31.7 1.7 collective-permute-done.1
  33.4 0.0 copy-done.4
  33.4 0.0 copy-done.5
  33.4 4.4 %pad_maximum_fusion.1 = bf16[2,6,12,256,128]{4,3,2,1,0:T(8,128)(2,1)} fusion(bf16[2,6,2,256,128]{4,3,2,1,0:T(8,128)(2,1)S(1)} %collective-permute-done.1, bf16[1,6,8,256,128]{4,3,2,1,0:T(8,128)(2,1)S(1)} %bitcast.21, bf16[1,6,8,256,128]{4,3,2,1,0:T(8,128)(2,1)S(1)} %bitcast.23, bf16[2,6,2,256,128]{4,3,2,1,0:T(8,128)(2,1)S(1)} %collective-permute-done), kind=kLoop, calls=%fused_computation.5 | loop fusion | flops 14155776 | bytes 18874368 | tf_op jit(solution)/shard_map/concatenate | solution.py:16
  37.8 12.8 %fusion.18 = (f32[6,12,256,128]{3,2,1,0:T(8,128)}, f32[6,12,256,128]{3,2,1,0:T(8,128)}) fusion(bf16[2,6,12,256,128]{4,3,2,1,0:T(8,128)(2,1)} %pad_maximum_fusion.1), kind=kLoop, calls=%fused_computation.34 | loop fusion | flops 4718592 | bytes 28311552 | tf_op jit(solution)/shard_map/convert_element_type | solution.py:51
  50.6 1.3 fusion.27
  51.9 0.0 copy-start.8
  51.9 15.6 %fusion.28 = (f32[6,8,255,128]{3,2,1,0:T(8,128)S(1)}, f32[6,8,255,128]{3,2,1,0:T(8,128)}, f32[6,8,255,128]{3,2,1,0:T(8,128)}, f32[6,8,255,128]{3,2,1,0:T(8,128)}) fusion(f32[6,12,256,128]{3,2,1,0:T(8,128)} %get-tuple-element.18, f32[6,12,256,128]{3,2,1,0:T(8,128)} %get-tuple-element.17), kind=kLoop, calls=%fused_computation.46 | loop fusion | bytes 50135040 | tf_op jit(solution)/shard_map/jit(_roll_static)/slice | solution.py:25
  67.6 0.0 copy-done.8
  67.6 27.2 %fusion.25 = (bf16[6,8,256,128]{3,2,1,0:T(8,128)(2,1)S(1)}, f32[6,8,256,128]{3,2,1,0:T(8,128)}, bf16[6,8,256,128]{3,2,1,0:T(8,128)(2,1)}) fusion(f32[6,12,256,128]{3,2,1,0:T(8,128)} %get-tuple-element.18, f32[6,8,255,128]{3,2,1,0:T(8,128)} %get-tuple-element.24, f32[6,8,1,128]{3,2,1,0:T(1,128)S(1)} %get-tuple-element.22, ...), kind=kLoop, calls=%fused_computation.44 | loop fusion | flops 44040192 | bytes 88088576 | tf_op jit(solution)/shard_map/convert.3
  94.8 9.8 %fusion.19 = (bf16[6,8,256,128]{3,2,1,0:T(8,128)(2,1)S(1)}, bf16[6,8,256,128]{3,2,1,0:T(8,128)(2,1)}) fusion(f32[6,8,256,128]{3,2,1,0:T(8,128)} %get-tuple-element.6, bf16[6,8,256,128]{3,2,1,0:T(8,128)(2,1)} %param.10, f32[8,256,128]{2,1,0:T(8,128)} %broadcast_multiply_fusion, f32[128]{0:T(128)S(1)} %copy-done.10, bf16[6,8,256,128]{3,2,1,0:T(8,128)(2,1)} %param.11), kind=kLoop, calls=%fused_computation.36 | loop fusion | flops 12582912 | bytes 19923456 | tf_op jit(solution)/shard_map/convert.5
  104.6 0.0 copy-done
  104.6 1.7 copy-done.6
  106.3 0.0 copy-done.2
  106.3 8.1 %fusion.20 = bf16[8,256,512]{2,1,0:T(8,128)(2,1)} fusion(bf16[6,8,256,128]{3,2,1,0:T(8,128)(2,1)} %get-tuple-element.8, bf16[6,8,256,128]{3,2,1,0:T(8,128)(2,1)S(1)} %get-tuple-element.7, bf16[6,8,256,128]{3,2,1,0:T(8,128)(2,1)S(1)} %copy-done.2, bf16[6,8,256,128]{3,2,1,0:T(8,128)(2,1)S(1)} %get-tuple-element.5), kind=kLoop, calls=%fused_computation.37 | loop fusion | flops 55574528 | bytes 14680064 | tf_op jit(solution)/shard_map/reduce_sum | solution.py:74
  114.4 0.0 all-reduce.3.cloned.1.call-update
  114.4 0.2 all-reduce.5.cloned.1.call-start
  114.6 130.1 %all-reduce.3.cloned.1.call-done = bf16[8,256,512]{2,1,0:T(8,128)(2,1)} async-done(((bf16[8,256,512]{2,1,0:T(8,128)(2,1)}), bf16[8,256,512]{2,1,0:T(8,128)(2,1)}) %all-reduce.3.cloned.1.call-update) | async-done | bytes 2097168 | tf_op jit(solution)/shard_map/psum | solution.py:76
  244.7 2.4 convert_multiply_fusion
  247.1 0.1 copy-done.3
  247.2 47.7 %fusion.21 = f32[512,512]{1,0:T(8,128)} fusion(f32[8,256,512]{2,1,0:T(8,128)S(1)} %convert_multiply_fusion, bf16[6,8,256,128]{3,2,1,0:T(8,128)(2,1)} %get-tuple-element.8, bf16[6,8,256,128]{3,2,1,0:T(8,128)(2,1)} %copy-done.6, bf16[6,8,256,128]{3,2,1,0:T(8,128)(2,1)S(1)} %copy-done.3, bf16[6,8,256,128]{3,2,1,0:T(8,128)(2,1)S(1)} %copy-done.1), kind=kOutput, calls=%fused_computation.40 | convolution fusion | flops 38711328768 | bytes 17825792 | tf_op jit(solution)/shard_map/dot_general | solution.py:29
  294.9 0.0 all-reduce.5.cloned.1.call-update
  294.9 94.7 %all-reduce.5.cloned.1.call-done = f32[512,512]{1,0:T(8,128)} async-done(((f32[512,512]{1,0:T(8,128)}), f32[512,512]{1,0:T(8,128)}) %all-reduce.5.cloned.1.call-update) | async-done | bytes 1048592 | tf_op jit(solution)/shard_map/psum | solution.py:79
  389.6 1.6 multiply_bitcast_fusion
  (12 shorter events, 0.0 us)
Async XLA Ops:
  6.5 26.9 %copy-start.4 = (bf16[6,8,256,128]{3,2,1,0:T(8,128)(2,1)S(1)}, bf16[6,8,256,128]{3,2,1,0:T(8,128)(2,1)}, u32[]{:S(2)}) copy-start(bf16[6,8,256,128]{3,2,1,0:T(8,128)(2,1)} %param.9) | copy-start | bytes 9437188
  6.5 8.9 %copy-start.7 = (f32[8,256]{1,0:T(8,128)S(1)}, f32[8,256]{1,0:T(8,128)}, u32[]{:S(2)}) copy-start(f32[8,256]{1,0:T(8,128)} %param.13) | copy-start | bytes 24580
  6.5 8.9 %copy-start.9 = (f32[128]{0:T(128)S(1)}, f32[128]{0:T(128)}, u32[]{:S(2)}) copy-start(f32[128]{0:T(128)} %param.14) | copy-start | bytes 1540
  6.5 238.2 %all-reduce.3.cloned.1.call-start = ((), (), s32[]{:S(2)}) async-start(), calls=%async_computation | async-start | bytes 4194304 | tf_op jit(solution)/shard_map/psum | solution.py:76
  6.5 26.9 %copy-start.5 = (bf16[6,8,256,128]{3,2,1,0:T(8,128)(2,1)S(1)}, bf16[6,8,256,128]{3,2,1,0:T(8,128)(2,1)}, u32[]{:S(2)}) copy-start(bf16[6,8,256,128]{3,2,1,0:T(8,128)(2,1)} %param.8) | copy-start | bytes 9437188
  8.8 22.9 %collective-permute-start = (bf16[2,6,2,256,128]{4,3,2,1,0:T(8,128)(2,1)S(1)}, bf16[2,6,2,256,128]{4,3,2,1,0:T(8,128)(2,1)S(1)}, u32[]{:S(2)}, u32[]{:S(2)}) collective-permute-start(bf16[2,6,2,256,128]{4,3,2,1,0:T(8,128)(2,1)S(1)} %get-tuple-element.19), channel_id=1, source_target_pairs={{0,1},{1,2},{2,3},{3,4},{4,5},{5,6},{6,7},{7,8},{8,9},{9,10},{10,1... | collective-permute-start | bytes 4718600 | tf_op jit(solution)/shard_map/ppermute | solution.py:12
  10.9 22.5 %collective-permute-start.1 = (bf16[2,6,2,256,128]{4,3,2,1,0:T(8,128)(2,1)S(1)}, bf16[2,6,2,256,128]{4,3,2,1,0:T(8,128)(2,1)S(1)}, u32[]{:S(2)}, u32[]{:S(2)}) collective-permute-start(bf16[2,6,2,256,128]{4,3,2,1,0:T(8,128)(2,1)S(1)} %get-tuple-element.20), channel_id=1, source_target_pairs={{1,0},{2,1},{3,2},{4,3},{5,4},{6,5},{7,6},{8,7},{9,8},{10,9},{11,1... | collective-permute-start | bytes 4718600 | tf_op jit(solution)/shard_map/ppermute | solution.py:15
  51.9 15.7 %copy-start.8 = (f32[8,256]{1,0:T(8,128)S(1)}, f32[8,256]{1,0:T(8,128)}, u32[]{:S(2)}) copy-start(f32[8,256]{1,0:T(8,128)} %param.12) | copy-start | bytes 24580
  67.6 27.2 %copy-start.10 = (f32[128]{0:T(128)S(1)}, f32[128]{0:T(128)}, u32[]{:S(2)}) copy-start(f32[128]{0:T(128)} %param.15) | copy-start | bytes 1540
  94.8 9.8 %copy-start = (bf16[6,8,256,128]{3,2,1,0:T(8,128)(2,1)}, bf16[6,8,256,128]{3,2,1,0:T(8,128)(2,1)S(1)}, u32[]{:S(2)}) copy-start(bf16[6,8,256,128]{3,2,1,0:T(8,128)(2,1)S(1)} %get-tuple-element.5) | copy-start | bytes 9437188
  94.8 11.5 %copy-start.2 = (bf16[6,8,256,128]{3,2,1,0:T(8,128)(2,1)S(1)}, bf16[6,8,256,128]{3,2,1,0:T(8,128)(2,1)}, u32[]{:S(2)}) copy-start(bf16[6,8,256,128]{3,2,1,0:T(8,128)(2,1)} %get-tuple-element.21) | copy-start | bytes 9437188
  104.6 1.7 copy-start.6
  114.4 132.7 %copy-start.1 = (bf16[6,8,256,128]{3,2,1,0:T(8,128)(2,1)S(1)}, bf16[6,8,256,128]{3,2,1,0:T(8,128)(2,1)}, u32[]{:S(2)}) copy-start(bf16[6,8,256,128]{3,2,1,0:T(8,128)(2,1)} %copy-done) | copy-start | bytes 9437188
  114.4 275.2 %all-reduce.5.cloned.1.call-start = ((), (), s32[]{:S(2)}) async-start(), calls=%async_computation.1 | async-start | bytes 2097152 | tf_op jit(solution)/shard_map/psum | solution.py:79
  244.7 2.5 copy-start.3
Sparse Core Ops, SparseCore 0:
  114.5 130.1 all-reduce.2
  295.0 94.4 all-reduce.4
where the time goes:
time: 398 us
  waiting for transfers between devices  241 us (61%)
  other arithmetic  69.8 us (18%)
  matrix products  47.7 us (12%)
  local copies, waits for them, and re-layouts  18.8 us (5%)
  between operations  13.5 us (3%)
  starting transfers between devices  6.82 us (2%)
    psum x1, waiting for transfers between devices, on_device(): lax.psum(local_sum.astype(jnp.bfloat16), 'member').astype(jnp.float32)  130 us
    psum x1, waiting for transfers between devices, on_device(): summed = lax.psum(gram_rows(anomaly, anomaly, highest), 'member')  94.7 us
    dot_general x1, matrix products, gram_rows(): lax.dot_general(left, right, (((0,), (0,)), ((), ())), preferred_element_...  47.7 us
    another operation x2, other arithmetic  37 us
    slice x2, local copies, waits for them, and re-layouts, lon_diff(): return (jnp.roll(field, -1, 2) - jnp.roll(field, 1, 2)) / 2.0  17 us
    ppermute x1, waiting for transfers between devices, extended(): lax.ppermute(lax.slice_in_dim(block, block.shape[dim] - width, None, axis...  14.9 us
    convert_element_type x1, other arithmetic, on_device(): v_full = padded[1].astype(jnp.float32)  12.8 us
    reduce_sum x1, other arithmetic, on_device(): local_sum = jnp.sum(sample_vector.astype(jnp.float32), axis=0)  8.08 us
  transfers between devices with their start and end apart: 4, of which 4 were waited for; matrix products, arithmetic and copies ran while one was open for 0% of the time, Pallas kernels for 0%

commit v1 on v0

--- a/solution.py
+++ b/solution.py
@@ -2,6 +2,12 @@
 import jax.numpy as jnp
 from jax import lax
 from jax.sharding import PartitionSpec as P
+from jax.lax import all_gather
+
+
+def update_kinds(shard_in):
+    met_up = all_gather(shard_in, "member").sum(axis=0)
+    return met_up
 
 
 def extended(block, sides, width):
@@ -76,7 +82,7 @@
     totals = lax.psum(local_sum.astype(jnp.bfloat16), "member").astype(jnp.float32)
     ens_mean = totals / members_all
     anomaly = (sample_vector.astype(jnp.float32) - ens_mean[None]).reshape(-1, width)
-    summed = lax.psum(gram_rows(anomaly, anomaly, highest), "member")
+    summed = update_kinds(gram_rows(anomaly, anomaly, highest))
     mine = lax.dynamic_slice_in_dim(summed, lax.axis_index("member") * rows, rows, 0)
     return (mine * scale)[None]
 

time: 398 us -> 419 us (1.053)
  waiting for transfers between devices: 241 us -> 257 us
    all_gather x0 -> x1, waiting for transfers between devices: none -> 111 us  [update_kinds(): met_up = all_gather(shard_in, 'member').sum(axis=0)]
    psum x1 -> x0, waiting for transfers between devices: 94.7 us -> none  [on_device(): summed = lax.psum(gram_rows(anomaly, anomaly, highest), 'member')]
    reduce_sum x0 -> x1, other arithmetic: none -> 4.49 us  [update_kinds(): met_up = all_gather(shard_in, 'member').sum(axis=0)]
where the time goes in v1:
time: 419 us; the launch traced here: 418 us
  waiting for transfers between devices  257 us (61%)
  other arithmetic  73.4 us (18%)
  matrix products  47.7 us (11%)
  local copies, waits for them, and re-layouts  18.8 us (4%)
  between operations  13.5 us (3%)
  starting transfers between devices  6.82 us (2%)
    psum x1, waiting for transfers between devices, on_device(): lax.psum(local_sum.astype(jnp.bfloat16), 'member').astype(jnp.float32)  130 us
    all_gather x1, waiting for transfers between devices, update_kinds(): met_up = all_gather(shard_in, 'member').sum(axis=0)  111 us
    dot_general x1, matrix products, gram_rows(): lax.dot_general(left, right, (((0,), (0,)), ((), ())), preferred_element_...  47.7 us
    another operation x2, other arithmetic  37 us
    slice x2, local copies, waits for them, and re-layouts, lon_diff(): return (jnp.roll(field, -1, 2) - jnp.roll(field, 1, 2)) / 2.0  17 us
    ppermute x1, waiting for transfers between devices, extended(): lax.ppermute(lax.slice_in_dim(block, block.shape[dim] - width, None, axis...  14.9 us
    convert_element_type x1, other arithmetic, on_device(): v_full = padded[1].astype(jnp.float32)  12.8 us
  transfers between devices with their start and end apart: 4, of which 4 were waited for; matrix products, arithmetic and copies ran while one was open for 0% of the time, Pallas kernels for 0%

profile of v1, /device:TPU:32, one launch (start us, length us, event | category | flops | bytes accessed | tf_op | source)
XLA Modules:
  0.0 417.7 jit_solution(14675721831401412600)
XLA Ops:
  6.5 0.0 all-reduce.2.cloned.1.call-start
  6.5 2.3 pad_maximum_fusion.4
  8.8 2.1 collective-permute-start
  10.9 4.5 %collective-permute-start.1 = (bf16[2,6,2,256,128]{4,3,2,1,0:T(8,128)(2,1)S(1)}, bf16[2,6,2,256,128]{4,3,2,1,0:T(8,128)(2,1)S(1)}, u32[]{:S(2)}, u32[]{:S(2)}) collective-permute-start(bf16[2,6,2,256,128]{4,3,2,1,0:T(8,128)(2,1)S(1)} %get-tuple-element.20), channel_id=1, source_target_pairs={{1,0},{2,1},{3,2},{4,3},{5,4},{6,5},{7,6},{8,7},{9,8},{10,9},{11,1... | collective-permute-start | bytes 4718600 | tf_op jit(solution)/shard_map/ppermute | solution.py:21
  15.4 0.0 copy-done.7
  15.4 0.0 copy-done.9
  15.5 1.3 broadcast_multiply_fusion
  16.8 14.9 %collective-permute-done = bf16[2,6,2,256,128]{4,3,2,1,0:T(8,128)(2,1)S(1)} collective-permute-done((bf16[2,6,2,256,128]{4,3,2,1,0:T(8,128)(2,1)S(1)}, bf16[2,6,2,256,128]{4,3,2,1,0:T(8,128)(2,1)S(1)}, u32[]{:S(2)}, u32[]{:S(2)}) %collective-permute-start) | collective-permute-done | bytes 1572896 | tf_op jit(solution)/shard_map/ppermute | solution.py:18
  31.7 1.7 collective-permute-done.1
  33.4 0.0 copy-done.4
  33.4 4.4 %pad_maximum_fusion.1 = bf16[2,6,12,256,128]{4,3,2,1,0:T(8,128)(2,1)} fusion(bf16[2,6,2,256,128]{4,3,2,1,0:T(8,128)(2,1)S(1)} %collective-permute-done.1, bf16[1,6,8,256,128]{4,3,2,1,0:T(8,128)(2,1)S(1)} %bitcast.22, bf16[1,6,8,256,128]{4,3,2,1,0:T(8,128)(2,1)S(1)} %bitcast.24, bf16[2,6,2,256,128]{4,3,2,1,0:T(8,128)(2,1)S(1)} %collective-permute-done), kind=kLoop, calls=%fused_computation.5 | loop fusion | flops 14155776 | bytes 18874368 | tf_op jit(solution)/shard_map/concatenate | solution.py:22
  37.8 12.8 %fusion.18 = (f32[6,12,256,128]{3,2,1,0:T(8,128)}, f32[6,12,256,128]{3,2,1,0:T(8,128)}) fusion(bf16[2,6,12,256,128]{4,3,2,1,0:T(8,128)(2,1)} %pad_maximum_fusion.1), kind=kLoop, calls=%fused_computation.34 | loop fusion | flops 4718592 | bytes 28311552 | tf_op jit(solution)/shard_map/convert_element_type | solution.py:57
  50.6 1.3 fusion.27
  51.9 0.0 copy-start.8
  51.9 15.6 %fusion.28 = (f32[6,8,255,128]{3,2,1,0:T(8,128)S(1)}, f32[6,8,255,128]{3,2,1,0:T(8,128)}, f32[6,8,255,128]{3,2,1,0:T(8,128)}, f32[6,8,255,128]{3,2,1,0:T(8,128)}) fusion(f32[6,12,256,128]{3,2,1,0:T(8,128)} %get-tuple-element.18, f32[6,12,256,128]{3,2,1,0:T(8,128)} %get-tuple-element.17), kind=kLoop, calls=%fused_computation.46 | loop fusion | bytes 50135040 | tf_op jit(solution)/shard_map/jit(_roll_static)/slice | solution.py:31
  67.6 0.0 copy-done.8
  67.6 27.2 %fusion.25 = (bf16[6,8,256,128]{3,2,1,0:T(8,128)(2,1)S(1)}, f32[6,8,256,128]{3,2,1,0:T(8,128)}, bf16[6,8,256,128]{3,2,1,0:T(8,128)(2,1)}) fusion(f32[6,12,256,128]{3,2,1,0:T(8,128)} %get-tuple-element.18, f32[6,8,255,128]{3,2,1,0:T(8,128)} %get-tuple-element.24, f32[6,8,1,128]{3,2,1,0:T(1,128)S(1)} %get-tuple-element.22, ...), kind=kLoop, calls=%fused_computation.44 | loop fusion | flops 44040192 | bytes 88088576 | tf_op jit(solution)/shard_map/convert.3
  94.8 9.8 %fusion.19 = (bf16[6,8,256,128]{3,2,1,0:T(8,128)(2,1)S(1)}, bf16[6,8,256,128]{3,2,1,0:T(8,128)(2,1)}) fusion(f32[6,8,256,128]{3,2,1,0:T(8,128)} %get-tuple-element.6, bf16[6,8,256,128]{3,2,1,0:T(8,128)(2,1)} %param.10, f32[8,256,128]{2,1,0:T(8,128)} %broadcast_multiply_fusion, f32[128]{0:T(128)S(1)} %copy-done.10, bf16[6,8,256,128]{3,2,1,0:T(8,128)(2,1)} %param.11), kind=kLoop, calls=%fused_computation.36 | loop fusion | flops 12582912 | bytes 19923456 | tf_op jit(solution)/shard_map/convert.5
  104.6 0.0 copy-done
  104.6 1.7 copy-done.6
  106.3 0.0 copy-done.2
  106.3 8.1 %fusion.20 = bf16[8,256,512]{2,1,0:T(8,128)(2,1)} fusion(bf16[6,8,256,128]{3,2,1,0:T(8,128)(2,1)} %get-tuple-element.8, bf16[6,8,256,128]{3,2,1,0:T(8,128)(2,1)S(1)} %get-tuple-element.7, bf16[6,8,256,128]{3,2,1,0:T(8,128)(2,1)S(1)} %copy-done.2, bf16[6,8,256,128]{3,2,1,0:T(8,128)(2,1)S(1)} %get-tuple-element.5), kind=kLoop, calls=%fused_computation.37 | loop fusion | flops 55574528 | bytes 14680064 | tf_op jit(solution)/shard_map/reduce_sum | solution.py:80
  114.4 0.0 all-reduce.2.cloned.1.call-update
  114.4 0.2 all-gather.3.cloned.1.call-start
  114.6 130.1 %all-reduce.2.cloned.1.call-done = bf16[8,256,512]{2,1,0:T(8,128)(2,1)} async-done(((bf16[8,256,512]{2,1,0:T(8,128)(2,1)}), bf16[8,256,512]{2,1,0:T(8,128)(2,1)}) %all-reduce.2.cloned.1.call-update) | async-done | bytes 2097168 | tf_op jit(solution)/shard_map/psum | solution.py:82
  244.7 2.4 convert_multiply_fusion
  247.1 0.1 copy-done.3
  247.2 47.7 %fusion.21 = f32[512,512]{1,0:T(8,128)} fusion(f32[8,256,512]{2,1,0:T(8,128)S(1)} %convert_multiply_fusion, bf16[6,8,256,128]{3,2,1,0:T(8,128)(2,1)} %get-tuple-element.8, bf16[6,8,256,128]{3,2,1,0:T(8,128)(2,1)} %copy-done.6, bf16[6,8,256,128]{3,2,1,0:T(8,128)(2,1)S(1)} %copy-done.3, bf16[6,8,256,128]{3,2,1,0:T(8,128)(2,1)S(1)} %copy-done.1), kind=kOutput, calls=%fused_computation.40 | convolution fusion | flops 38711328768 | bytes 17825792 | tf_op jit(solution)/shard_map/dot_general | solution.py:35
  295.0 0.0 all-gather.3.cloned.1.call-update
  295.0 110.7 %all-gather.3.cloned.1.call-done = f32[4096,512]{1,0:T(8,128)} async-done(((f32[512,512]{1,0:T(8,128)}), f32[4096,512]{1,0:T(8,128)}) %all-gather.3.cloned.1.call-update) | async-done | bytes 8388624 | tf_op jit(solution)/shard_map/all_gather | solution.py:9
  405.7 4.5 %reduce_sum.22 = f32[512,512]{1,0:T(8,128)S(1)} reduce(f32[8,512,512]{2,1,0:T(8,128)} %bitcast.25, f32[]{:T(128)} %constant.24.clone.1), dimensions={0}, to_apply=%region_2.3 | reduce | flops 1835008 | bytes 9437188 | tf_op jit(solution)/shard_map/reduce_sum | solution.py:9
  410.2 0.7 multiply_bitcast_fusion
  (13 shorter events, 0.0 us)
Async XLA Ops:
  6.5 26.9 %copy-start.4 = (bf16[6,8,256,128]{3,2,1,0:T(8,128)(2,1)S(1)}, bf16[6,8,256,128]{3,2,1,0:T(8,128)(2,1)}, u32[]{:S(2)}) copy-start(bf16[6,8,256,128]{3,2,1,0:T(8,128)(2,1)} %param.9) | copy-start | bytes 9437188
  6.5 8.9 %copy-start.7 = (f32[8,256]{1,0:T(8,128)S(1)}, f32[8,256]{1,0:T(8,128)}, u32[]{:S(2)}) copy-start(f32[8,256]{1,0:T(8,128)} %param.13) | copy-start | bytes 24580
  6.5 8.9 %copy-start.9 = (f32[128]{0:T(128)S(1)}, f32[128]{0:T(128)}, u32[]{:S(2)}) copy-start(f32[128]{0:T(128)} %param.14) | copy-start | bytes 1540
  6.5 238.2 %all-reduce.2.cloned.1.call-start = ((), (), s32[]{:S(2)}) async-start(), calls=%async_computation | async-start | bytes 4194304 | tf_op jit(solution)/shard_map/psum | solution.py:82
  6.5 26.9 %copy-start.5 = (bf16[6,8,256,128]{3,2,1,0:T(8,128)(2,1)S(1)}, bf16[6,8,256,128]{3,2,1,0:T(8,128)(2,1)}, u32[]{:S(2)}) copy-start(bf16[6,8,256,128]{3,2,1,0:T(8,128)(2,1)} %param.8) | copy-start | bytes 9437188
  8.8 22.9 %collective-permute-start = (bf16[2,6,2,256,128]{4,3,2,1,0:T(8,128)(2,1)S(1)}, bf16[2,6,2,256,128]{4,3,2,1,0:T(8,128)(2,1)S(1)}, u32[]{:S(2)}, u32[]{:S(2)}) collective-permute-start(bf16[2,6,2,256,128]{4,3,2,1,0:T(8,128)(2,1)S(1)} %get-tuple-element.19), channel_id=1, source_target_pairs={{0,1},{1,2},{2,3},{3,4},{4,5},{5,6},{6,7},{7,8},{8,9},{9,10},{10,1... | collective-permute-start | bytes 4718600 | tf_op jit(solution)/shard_map/ppermute | solution.py:18
  10.9 22.5 %collective-permute-start.1 = (bf16[2,6,2,256,128]{4,3,2,1,0:T(8,128)(2,1)S(1)}, bf16[2,6,2,256,128]{4,3,2,1,0:T(8,128)(2,1)S(1)}, u32[]{:S(2)}, u32[]{:S(2)}) collective-permute-start(bf16[2,6,2,256,128]{4,3,2,1,0:T(8,128)(2,1)S(1)} %get-tuple-element.20), channel_id=1, source_target_pairs={{1,0},{2,1},{3,2},{4,3},{5,4},{6,5},{7,6},{8,7},{9,8},{10,9},{11,1... | collective-permute-start | bytes 4718600 | tf_op jit(solution)/shard_map/ppermute | solution.py:21
  51.9 15.7 %copy-start.8 = (f32[8,256]{1,0:T(8,128)S(1)}, f32[8,256]{1,0:T(8,128)}, u32[]{:S(2)}) copy-start(f32[8,256]{1,0:T(8,128)} %param.12) | copy-start | bytes 24580
  67.6 27.2 %copy-start.10 = (f32[128]{0:T(128)S(1)}, f32[128]{0:T(128)}, u32[]{:S(2)}) copy-start(f32[128]{0:T(128)} %param.15) | copy-start | bytes 1540
  94.8 9.8 %copy-start = (bf16[6,8,256,128]{3,2,1,0:T(8,128)(2,1)}, bf16[6,8,256,128]{3,2,1,0:T(8,128)(2,1)S(1)}, u32[]{:S(2)}) copy-start(bf16[6,8,256,128]{3,2,1,0:T(8,128)(2,1)S(1)} %get-tuple-element.5) | copy-start | bytes 9437188
  94.8 11.5 %copy-start.2 = (bf16[6,8,256,128]{3,2,1,0:T(8,128)(2,1)S(1)}, bf16[6,8,256,128]{3,2,1,0:T(8,128)(2,1)}, u32[]{:S(2)}) copy-start(bf16[6,8,256,128]{3,2,1,0:T(8,128)(2,1)} %get-tuple-element.21) | copy-start | bytes 9437188
  104.6 1.7 copy-start.6
  114.4 132.7 %copy-start.1 = (bf16[6,8,256,128]{3,2,1,0:T(8,128)(2,1)S(1)}, bf16[6,8,256,128]{3,2,1,0:T(8,128)(2,1)}, u32[]{:S(2)}) copy-start(bf16[6,8,256,128]{3,2,1,0:T(8,128)(2,1)} %copy-done) | copy-start | bytes 9437188
  114.4 291.3 %all-gather.3.cloned.1.call-start = ((), (), s32[]{:S(2)}) async-start(), calls=%async_computation.1 | async-start | bytes 9437184 | tf_op jit(solution)/shard_map/all_gather | solution.py:9
  244.7 2.5 copy-start.3
Sparse Core Ops, SparseCore 0:
  114.5 130.1 all-reduce.1
  295.1 110.5 all-gather.2
